TPU v7x, 32 devices: a whole 2x2x4 slice. The times are simulated.
32 devices in a mesh: grp: 2 (over y), smp: 4 (over z), st: 2 (over x), sub: 2 (over core).
Axes of the slice: x: 2, y: 2, z: 4, core: 2. Of those that a mesh axis runs over, the one named last changes fastest.
Arguments:
- energies: float32 [3072, 2048], P(('grp', 'smp'), ('st', 'sub')), parts along dimension 0, may hold values from -300 to 300
- counts: int32 [4096], P(('grp', 'st', 'sub')), parts along dimension 0, may hold values from 16 to 48
- labels: int32 [3072], P(('grp', 'smp')), parts along dimension 0, may hold values from 0 to 2047
Outputs:
- start_energy: float32 [4096], P(('grp', 'st', 'sub')), parts along dimension 0
- free_energy: float32 [4096], P(('grp', 'st', 'sub')), parts along dimension 0
- correlation: float32 [4096, 2048], P(('grp', 'smp'), ('st', 'sub')), parts along dimension 0
There are 2 independent parts, one for each index of `grp`. A program takes and returns all parts, laid end to end along the dimension named above; each array names one. Nothing has to cross between parts.
All inputs are finite; a program needn't handle non-finite values.
Results may differ from a plain program's by a relative error of at most 0.0003.
Values sent between devices are 32-bit elements; how exact they have to be, the bound alone decides.
A program may use at most 64 MiB of HBM per device.

v0:
```python
import jax
import jax.numpy as jnp
from jax import lax
from jax.sharding import PartitionSpec as P

ITERS = 3


def sample_lse(scores):
    local_peak = jnp.max(scores, axis=1)
    row_peak = lax.pmax(local_peak, ("st", "sub"))
    row_total = lax.psum(jnp.sum(jnp.exp(scores - row_peak[:, None]), axis=1), ("st", "sub"))
    return row_peak + jnp.log(row_total)


def state_lse(scores):
    local_peak = jnp.max(scores, axis=0)
    col_peak = lax.pmax(local_peak, "smp")
    col_total = lax.psum(jnp.sum(jnp.exp(scores - col_peak[None, :]), axis=0), "smp")
    return col_peak + jnp.log(col_total)


def per_device(energies, counts, labels):
    local_states = energies.shape[1]
    total_states = local_states * lax.axis_size(("st", "sub"))
    first_state = lax.axis_index(("st", "sub")) * local_states
    state_ids = first_state + jnp.arange(local_states, dtype=jnp.int32)
    anchor_hit = labels[:, None] == state_ids[None, :]
    energy_sums, label_counts = lax.psum(
        (
            jnp.sum(jnp.where(anchor_hit, energies, jnp.float32(0.0)), axis=0),
            jnp.sum(anchor_hit.astype(jnp.float32), axis=0),
        ),
        "smp",
    )
    start_energy = energy_sums / jnp.maximum(label_counts, jnp.float32(1.0))
    free_energy = start_energy
    log_counts = jnp.log(counts.astype(jnp.float32))
    for iteration in range(ITERS):
        log_denom = sample_lse(log_counts[None, :] + free_energy[None, :] - energies)
        free_energy = -state_lse(-energies - log_denom[:, None])
    log_denom = sample_lse(log_counts[None, :] + free_energy[None, :] - energies)
    weights = jnp.exp(free_energy[None, :] - energies - log_denom[:, None])
    all_states = lax.all_gather(weights, ("st", "sub"), axis=1, tiled=True)
    gram_block = lax.psum_scatter(
        lax.dot_general(
            all_states,
            weights,
            (((0,), (0,)), ((), ())),
            precision=lax.Precision.HIGHEST,
            preferred_element_type=jnp.float32,
        ),
        "smp",
        scatter_dimension=0,
        tiled=True,
    )
    correlation = (jnp.float32(total_states) * counts.astype(jnp.float32))[None, :] * gram_block
    return (start_energy, free_energy, correlation)


def solution(mesh):
    return jax.shard_map(
        per_device,
        mesh=mesh,
        in_specs=(P(("grp", "smp"), ("st", "sub")), P(("grp", "st", "sub")), P(("grp", "smp"))),
        out_specs=(
            P(("grp", "st", "sub")),
            P(("grp", "st", "sub")),
            P(("grp", "smp"), ("st", "sub")),
        ),
        check_vma=False,
    )
```

profile of v0, /device:TPU:3, one launch (start us, length us, event | category | flops | bytes accessed | tf_op | source)
XLA Modules:
  0.0 256.2 jit_solution(18367101329578772509)
XLA Ops:
  7.3 1.4 fusion.1
  8.7 9.9 %all-reduce = (f32[512]{0:T(512)S(1)}, f32[512]{0:T(512)S(1)}) all-reduce(f32[512]{0:T(512)S(1)} %get-tuple-element.4, f32[512]{0:T(512)S(1)} %get-tuple-element.3), channel_id=1, replica_groups=mesh['grp'=2,'smp'=4,'st'=2,'sub'=2] {'smp'}, use_global_device_ids=true, to_apply=%region_1.2 | all-reduce | flops 1024 | bytes 8192 | tf_op jit(solution)/shard_map/psum | solution.py:29
  18.6 1.3 fusion.3
  19.9 1.3 subtract_reduce_fusion.6
  21.2 7.8 %pmax.49 = f32[384]{0:T(512)S(1)} all-reduce(f32[384]{0:T(512)S(1)} %subtract_reduce_fusion.6), channel_id=1, replica_groups=mesh['grp'=2,'smp'=4,'st'=2,'sub'=2] {'st','sub'}, use_global_device_ids=true, to_apply=%region_5.6 | all-reduce | flops 384 | bytes 3072 | tf_op jit(solution)/shard_map/pmax | solution.py:11
  28.9 1.4 exponential_reduce_fusion.6
  30.3 5.9 %psum.65 = f32[384]{0:T(512)S(1)} all-reduce(f32[384]{0:T(512)S(1)} %exponential_reduce_fusion.6), channel_id=1, replica_groups=mesh['grp'=2,'smp'=4,'st'=2,'sub'=2] {'st','sub'}, use_global_device_ids=true, to_apply=%region_7.8 | all-reduce | flops 384 | bytes 3072 | tf_op jit(solution)/shard_map/psum | solution.py:12
  36.3 1.3 subtract_reduce_fusion.5
  37.5 6.6 %pmax.50 = f32[512]{0:T(512)S(1)} all-reduce(f32[512]{0:T(512)S(1)} %subtract_reduce_fusion.5), channel_id=1, replica_groups=mesh['grp'=2,'smp'=4,'st'=2,'sub'=2] {'smp'}, use_global_device_ids=true, to_apply=%region_9.10 | all-reduce | flops 512 | bytes 4096 | tf_op jit(solution)/shard_map/pmax | solution.py:18
  44.4 8.1 %psum.66 = f32[512]{0:T(512)S(1)} all-reduce(f32[512]{0:T(512)S(1)} %exponential_reduce_fusion.5), channel_id=1, replica_groups=mesh['grp'=2,'smp'=4,'st'=2,'sub'=2] {'smp'}, use_global_device_ids=true, to_apply=%region_11.12 | all-reduce | flops 512 | bytes 4096 | tf_op jit(solution)/shard_map/psum | solution.py:19
  52.7 9.8 %pmax.51 = f32[384]{0:T(512)S(1)} all-reduce(f32[384]{0:T(512)S(1)} %subtract_reduce_fusion.4), channel_id=1, replica_groups=mesh['grp'=2,'smp'=4,'st'=2,'sub'=2] {'st','sub'}, use_global_device_ids=true, to_apply=%region_13.14 | all-reduce | flops 384 | bytes 3072 | tf_op jit(solution)/shard_map/pmax | solution.py:11
  62.8 5.7 %psum.67 = f32[384]{0:T(512)S(1)} all-reduce(f32[384]{0:T(512)S(1)} %exponential_reduce_fusion.4), channel_id=1, replica_groups=mesh['grp'=2,'smp'=4,'st'=2,'sub'=2] {'st','sub'}, use_global_device_ids=true, to_apply=%region_15.16 | all-reduce | flops 384 | bytes 3072 | tf_op jit(solution)/shard_map/psum | solution.py:12
  68.6 6.6 %pmax.52 = f32[512]{0:T(512)S(1)} all-reduce(f32[512]{0:T(512)S(1)} %subtract_reduce_fusion.3), channel_id=1, replica_groups=mesh['grp'=2,'smp'=4,'st'=2,'sub'=2] {'smp'}, use_global_device_ids=true, to_apply=%region_17.18 | all-reduce | flops 512 | bytes 4096 | tf_op jit(solution)/shard_map/pmax | solution.py:18
  75.5 8.1 %psum.68 = f32[512]{0:T(512)S(1)} all-reduce(f32[512]{0:T(512)S(1)} %exponential_reduce_fusion.3), channel_id=1, replica_groups=mesh['grp'=2,'smp'=4,'st'=2,'sub'=2] {'smp'}, use_global_device_ids=true, to_apply=%region_19.20 | all-reduce | flops 512 | bytes 4096 | tf_op jit(solution)/shard_map/psum | solution.py:19
  83.7 10.5 %pmax.53 = f32[384]{0:T(512)S(1)} all-reduce(f32[384]{0:T(512)S(1)} %subtract_reduce_fusion.2), channel_id=1, replica_groups=mesh['grp'=2,'smp'=4,'st'=2,'sub'=2] {'st','sub'}, use_global_device_ids=true, to_apply=%region_21.22 | all-reduce | flops 384 | bytes 3072 | tf_op jit(solution)/shard_map/pmax | solution.py:11
  94.6 5.7 %psum.69 = f32[384]{0:T(512)S(1)} all-reduce(f32[384]{0:T(512)S(1)} %exponential_reduce_fusion.2), channel_id=1, replica_groups=mesh['grp'=2,'smp'=4,'st'=2,'sub'=2] {'st','sub'}, use_global_device_ids=true, to_apply=%region_23.24 | all-reduce | flops 384 | bytes 3072 | tf_op jit(solution)/shard_map/psum | solution.py:12
  100.4 6.6 %pmax.54 = f32[512]{0:T(512)S(1)} all-reduce(f32[512]{0:T(512)S(1)} %subtract_reduce_fusion.1), channel_id=1, replica_groups=mesh['grp'=2,'smp'=4,'st'=2,'sub'=2] {'smp'}, use_global_device_ids=true, to_apply=%region_25.26 | all-reduce | flops 512 | bytes 4096 | tf_op jit(solution)/shard_map/pmax | solution.py:18
  107.3 8.1 %psum.70 = f32[512]{0:T(512)S(1)} all-reduce(f32[512]{0:T(512)S(1)} %exponential_reduce_fusion.1), channel_id=1, replica_groups=mesh['grp'=2,'smp'=4,'st'=2,'sub'=2] {'smp'}, use_global_device_ids=true, to_apply=%region_27.28 | all-reduce | flops 512 | bytes 4096 | tf_op jit(solution)/shard_map/psum | solution.py:19
  115.5 10.3 %pmax.55 = f32[384]{0:T(512)S(1)} all-reduce(f32[384]{0:T(512)S(1)} %subtract_reduce_fusion), channel_id=1, replica_groups=mesh['grp'=2,'smp'=4,'st'=2,'sub'=2] {'st','sub'}, use_global_device_ids=true, to_apply=%region_29.30 | all-reduce | flops 384 | bytes 3072 | tf_op jit(solution)/shard_map/pmax | solution.py:11
  126.1 5.7 %psum.71 = f32[384]{0:T(512)S(1)} all-reduce(f32[384]{0:T(512)S(1)} %exponential_reduce_fusion), channel_id=1, replica_groups=mesh['grp'=2,'smp'=4,'st'=2,'sub'=2] {'st','sub'}, use_global_device_ids=true, to_apply=%region_31.32 | all-reduce | flops 384 | bytes 3072 | tf_op jit(solution)/shard_map/psum | solution.py:12
  132.9 26.9 %all-gather.2.cloned.1.call-done = f32[384,2048]{1,0:T(8,128)} async-done(((f32[384,512]{1,0:T(8,128)}), f32[384,2048]{1,0:T(8,128)}) %all-gather.2.cloned.1.call-update) | async-done | bytes 3145744 | tf_op jit(solution)/shard_map/all_gather | solution.py:44
  159.8 9.8 %fusion.4 = f32[2048,512]{1,0:T(8,128)} fusion(f32[384,2048]{1,0:T(8,128)} %all-gather.2.cloned.1.call-done, f32[384,512]{1,0:T(8,128)} %subtract_exponential_fusion), kind=kOutput, calls=%fused_computation.33 | convolution fusion | flops 4831838208 | bytes 8126464 | tf_op jit(solution)/shard_map/dot_general | solution.py:46
  169.7 77.4 %reduce-scatter.2.cloned.1.call-done = f32[512,512]{1,0:T(8,128)} async-done(((f32[2048,512]{1,0:T(8,128)}), f32[512,512]{1,0:T(8,128)}) %reduce-scatter.2.cloned.1.call-update) | async-done | bytes 1048592 | tf_op jit(solution)/shard_map/reduce_scatter | solution.py:45
  247.1 2.3 broadcast_multiply_fusion
  (30 shorter events, 3.6 us)
Async XLA Ops:
  7.2 37.0 %copy-start = (f32[384,512]{1,0:T(8,128)S(1)}, f32[384,512]{1,0:T(8,128)}, u32[]{:S(2)}) copy-start(f32[384,512]{1,0:T(8,128)} %param.3) | copy-start | bytes 2359300
  7.2 45.3 %copy-start.1 = (s32[512]{0:T(512)S(1)}, s32[512]{0:T(512)}, u32[]{:S(2)}) copy-start(s32[512]{0:T(512)} %param.4) | copy-start | bytes 6148
  7.2 152.6 %all-gather.2.cloned.1.call-start = ((), (), s32[]{:S(2)}) async-start(), calls=%async_computation.1 | async-start | bytes 3932160 | tf_op jit(solution)/shard_map/all_gather | solution.py:44
  115.4 54.3 %copy-start.2 = (f32[512]{0:T(512)}, f32[512]{0:T(512)S(1)}, u32[]{:S(2)}) copy-start(f32[512]{0:T(512)S(1)} %get-tuple-element.8) | copy-start | bytes 6148
  132.9 114.2 %reduce-scatter.2.cloned.1.call-start = ((), (), s32[]{:S(2)}) async-start(), calls=%async_computation.2 | async-start | bytes 5242880 | tf_op jit(solution)/shard_map/reduce_scatter | solution.py:45
Sparse Core Ops, SparseCore 0:
  133.0 26.7 all-gather.1
  169.8 77.2 reduce-scatter.1
where the time goes:
time: 259 us; the launch traced here: 256 us
  blocking collectives  115 us (44%)
  waiting for transfers between devices  104 us (40%)
  between operations  14.1 us (5%)
  other arithmetic  12.5 us (5%)
  matrix products  9.84 us (4%)
    reduce_scatter x1, waiting for transfers between devices, per_device(): lax.psum_scatter(lax.dot_general(all_states, weights, (((0,), (0,)), ((),...  77.4 us
    pmax x4, blocking collectives, sample_lse(): row_peak = lax.pmax(local_peak, ('st', 'sub'))  38.4 us
    all_gather x1, waiting for transfers between devices, per_device(): all_states = lax.all_gather(weights, ('st', 'sub'), axis=1, tiled=True)  26.9 us
    psum x3, blocking collectives, state_lse(): lax.psum(jnp.sum(jnp.exp(scores - col_peak[None, :]), axis=0), 'smp')  24.2 us
    psum x4, blocking collectives, sample_lse(): lax.psum(jnp.sum(jnp.exp(scores - row_peak[:, None]), axis=1), ('st', 'su...  22.9 us
    pmax x3, blocking collectives, state_lse(): col_peak = lax.pmax(local_peak, 'smp')  19.9 us
    psum x1, blocking collectives, per_device(): lax.psum((jnp.sum(jnp.where(anchor_hit, energies, jnp.float32(0.0)), axis...  9.95 us
    dot_general x1, matrix products, per_device(): lax.dot_general(all_states, weights, (((0,), (0,)), ((), ())), precision=...  9.84 us
  transfers between devices with their start and end apart: 2, of which 2 were waited for; matrix products, arithmetic and copies ran while one was open for 0% of the time, Pallas kernels for 0%

commit v1 on v0

v1 whole, which is shorter than its diff:
```python
import functools

import jax
import jax.numpy as jnp
from jax import lax
from jax.experimental import pallas as pl
from jax.experimental.pallas import tpu as pltpu
from jax.sharding import PartitionSpec as P

ITERS = 3
LANES = 128
HAND, RELAY, LAND = 2, 2, 1
MESH = pl.DeviceIdType.MESH


def to_lanes(col):
    return jnp.transpose(jnp.broadcast_to(col, (col.shape[0], LANES)))[0:1, :]


def to_rows(row, width):
    tall = jnp.transpose(jnp.broadcast_to(row, (LANES, row.shape[1])))
    return jnp.concatenate([tall] * (width // LANES), axis=1)


def lse_of(parts):
    peak = functools.reduce(jnp.maximum, parts)
    return peak + jnp.log(sum(jnp.exp(part - peak) for part in parts))


def split(values):
    high = values.astype(jnp.bfloat16)
    return high, (values - high.astype(jnp.float32)).astype(jnp.bfloat16)


def pairs(left, right):
    return lax.dot_general(
        left, right, (((0,), (0,)), ((), ())), preferred_element_type=jnp.float32
    )


def kernel(
    n, n_st, n_sub, chunks, rows_out,
    e_hbm, counts_ref, labels_ref, start_ref, free_ref, gram_ref,
    eall, erow, acc, sbuf, zbuf, xbuf, fbuf, lbuf,
    load_sem, zs, zr, xs, xr, bs, br, rs, rr,
):
    samples, width = eall.shape[1], eall.shape[2]
    window = erow.shape[2]
    nq = n_st * n_sub
    p, st, sub = lax.axis_index("smp"), lax.axis_index("st"), lax.axis_index("sub")
    q = st * n_sub + sub
    piece = samples // chunks
    ticks = (n - 1) * chunks
    lags = HAND + RELAY + LAND

    first_row = p * rows_out
    owner = lax.div(first_row, width)
    owner_st, owner_sub = lax.div(owner, n_sub), lax.rem(owner, n_sub)
    in_block = lax.rem(first_row, width)
    lane0 = pl.multiple_of(lax.div(in_block, window) * window, LANES)
    is_owner = jnp.logical_and(st == owner_st, sub == owner_sub)
    is_relay = jnp.logical_and(st != owner_st, sub == owner_sub)
    is_end = sub != owner_sub

    load = pltpu.make_async_copy(e_hbm, eall.at[p], load_sem)
    load.start()
    barrier = pltpu.get_barrier_semaphore()
    for k in range(1, n):
        pl.semaphore_signal(
            barrier, inc=1, device_id={"smp": lax.rem(p + k, n)}, device_id_type=MESH
        )

    def plane(k):
        peer = lax.rem(q + k, nq)
        return {"st": lax.div(peer, n_sub), "sub": lax.rem(peer, n_sub)}

    for k in range(1, nq):
        pl.semaphore_signal(barrier, inc=1, device_id=plane(k), device_id_type=MESH)
    pl.semaphore_wait(barrier, n - 1 + nq - 1)
    load.wait()

    def remote(src, dst, send, recv, where):
        return pltpu.make_async_remote_copy(
            src_ref=src, dst_ref=dst, send_sem=send, recv_sem=recv,
            device_id=where, device_id_type=MESH,
        )

    def z_copy(buf, phase, k, slot):
        return remote(
            buf.at[p], buf.at[slot], zs.at[phase, k], zr.at[phase, k],
            {"smp": lax.rem(p + k, n)},
        )

    def z_send(buf, phase):
        for k in range(n - 1, 0, -1):
            z_copy(buf, phase, k, p).start()

    def z_recv(buf, phase):
        for k in range(1, n):
            z_copy(buf, phase, k, lax.rem(p + n - k, n)).wait_recv()

    def x_copy(buf, phase, k, slot):
        return remote(buf.at[q], buf.at[slot], xs.at[phase, k], xr.at[phase, k], plane(k))

    def x_send(buf, phase):
        for k in range(1, nq):
            x_copy(buf, phase, k, q).start()

    def x_recv(buf, phase):
        for k in range(1, nq):
            x_copy(buf, phase, k, lax.rem(q + nq - k, nq)).wait_recv()

    def rows_of(c):
        return pl.ds(pl.multiple_of(c * piece, 8), piece)

    def bulk(way, t, block):
        view = eall.at[block, rows_of(lax.rem(t, chunks))]
        return remote(
            view, view, bs.at[way, t], br.at[way, t], {"smp": p + 1 if way == 0 else p - 1}
        )

    def sends(t):
        hop = lax.div(t, chunks)
        return (
            (0, p - hop, jnp.logical_and(p < n - 1, hop <= p)),
            (1, p + hop, jnp.logical_and(p > 0, hop <= n - 1 - p)),
        )

    def arrivals(t):
        hop = lax.div(t, chunks)
        good = t >= 0
        return (
            (0, p - 1 - hop, jnp.logical_and(good, hop <= p - 1)),
            (1, p + 1 + hop, jnp.logical_and(good, hop <= n - 2 - p)),
        )

    def events(t):
        own = jnp.logical_and(t >= 0, t < chunks)
        return ((None, p, own),) + arrivals(t)

    def row_local(block, c):
        src = eall.at[block, rows_of(c)]
        if window != width:
            src = eall.at[block, rows_of(c), pl.ds(lane0, window)]
        return pltpu.make_async_copy(src, erow.at[block, rows_of(c)], rr.at[block, c])

    def row_first(block, c, peer):
        src = eall.at[block, rows_of(c)]
        if window != width:
            src = eall.at[block, rows_of(c), pl.ds(lane0, window)]
        where = (
            {"st": lax.rem(st + peer, n_st)}
            if peer < n_st
            else {"sub": lax.rem(sub + peer - n_st + 1, n_sub)}
        )
        return remote(
            src, erow.at[block, rows_of(c)], rs.at[peer - 1, block, c], rr.at[block, c], where
        )

    def row_again(block, c, peer):
        view = erow.at[block, rows_of(c)]
        return remote(
            view, view, rs.at[peer - 1, block, c], rr.at[block, c],
            {"sub": lax.rem(sub + peer - n_st + 1, n_sub)},
        )

    first_peers = range(1, n_st + n_sub - 1)
    again_peers = range(n_st, n_st + n_sub - 1)

    def tick(t):
        t = jnp.int32(t)
        for way, block, good in sends(t):
            @pl.when(jnp.logical_and(good, t < ticks))
            def _():
                bulk(way, t, block).start()

        u = t - HAND
        c = lax.rem(u + chunks, chunks)
        for way, block, good in events(u):
            if way is not None:
                @pl.when(good)
                def _():
                    bulk(way, u, block).wait_recv()

            @pl.when(jnp.logical_and(good, is_owner))
            def _():
                for peer in first_peers:
                    row_first(block, c, peer).start()
                row_local(block, c).start()

        u2 = u - RELAY
        c2 = lax.rem(u2 + 2 * chunks, chunks)
        for way, block, good in events(u2):
            @pl.when(jnp.logical_and(good, is_owner))
            def _():
                row_local(block, c2).wait()

            @pl.when(jnp.logical_and(good, is_relay))
            def _():
                row_again(block, c2, again_peers[0] if again_peers else 1).wait_recv()
                for peer in again_peers:
                    row_again(block, c2, peer).start()

        u3 = u2 - LAND
        c3 = lax.rem(u3 + 6 * chunks, chunks)
        for way, block, good in events(u3):
            @pl.when(jnp.logical_and(good, is_end))
            def _():
                row_again(block, c3, n_st).wait_recv()

    plan = iter(range(10**6))

    energies = eall.at[p]
    label_rows = to_rows(labels_ref[...].astype(jnp.float32), width)
    state_ids = lax.broadcasted_iota(jnp.int32, (samples, width), 1) + q * width
    hit = label_rows == state_ids.astype(jnp.float32)
    sbuf[p, 0:1, :] = jnp.sum(jnp.where(hit, energies[...], jnp.float32(0.0)), axis=0, keepdims=True)
    sbuf[p, 1:2, :] = jnp.sum(hit.astype(jnp.float32), axis=0, keepdims=True)
    z_send(sbuf, 0)
    tick(next(plan))
    tick(next(plan))
    log_counts = jnp.log(counts_ref[...].astype(jnp.float32))
    z_recv(sbuf, 0)
    total = sum(sbuf[j] for j in range(n))
    start = total[0:1, :] / jnp.maximum(total[1:2, :], jnp.float32(1.0))
    start_ref[...] = start

    def row_lse(free, phase):
        scores = (log_counts + free) - energies[...]
        peak = jnp.max(scores, axis=1, keepdims=True)
        local = peak + jnp.log(jnp.sum(jnp.exp(scores - peak), axis=1, keepdims=True))
        here = xbuf.at[phase]
        here[q] = to_lanes(local)
        x_send(here, phase)
        tick(next(plan))
        x_recv(here, phase)
        return lse_of([here[j] for j in range(nq)])

    free = start
    for step in range(ITERS):
        denom = row_lse(free, step)
        scores = -energies[...] - to_rows(denom, width)
        peak = jnp.max(scores, axis=0, keepdims=True)
        local = peak + jnp.log(jnp.sum(jnp.exp(scores - peak), axis=0, keepdims=True))
        here = zbuf.at[step]
        here[p] = local
        z_send(here, step + 1)
        tick(next(plan))
        z_recv(here, step + 1)
        free = -lse_of([here[j] for j in range(n)])
    free_ref[...] = free
    fbuf[q] = free
    x_send(fbuf, ITERS + 1)
    denom = row_lse(free, ITERS)
    lbuf[p] = denom
    z_send(lbuf, ITERS + 1)
    tick(next(plan))
    acc[...] = jnp.zeros_like(acc)
    x_recv(fbuf, ITERS + 1)
    z_recv(lbuf, ITERS + 1)

    def add_block(block):
        denom_rows = to_rows(lbuf[block], LANES)
        row_free = fbuf[owner] if window == width else fbuf[owner, :, pl.ds(lane0, window)]

        def weights(free_row, view):
            wide = jnp.concatenate([denom_rows] * (view.shape[1] // LANES), axis=1)
            return split(
                jnp.exp(free_row - view[...] - wide)
            )

        col_high, col_low = weights(free_ref[...], eall.at[block])
        row_high, row_low = weights(row_free, erow.at[block])
        acc[...] += pairs(row_high, col_high) + (
            pairs(row_high, col_low) + pairs(row_low, col_high)
        )

    def add_hop(hop, carry):
        def side(s, inner):
            block = jnp.where(s == 0, p, jnp.where(s == 1, p - 1 - hop, p + 1 + hop))
            good = jnp.where(
                s == 0, hop == 0, jnp.where(s == 1, hop <= p - 1, hop <= n - 2 - p)
            )

            @pl.when(good)
            def _():
                add_block(block)

            return inner

        lax.fori_loop(0, 3, side, 0)
        return carry

    def tail(t, carry):
        tick(t)
        done = t - lags + 1

        @pl.when(jnp.logical_and(done > 0, lax.rem(done, chunks) == 0))
        def _():
            add_hop(lax.div(done, chunks) - 1, 0)

        return carry

    first = next(plan)
    ready = min(max(0, (first - lags) // chunks), n - 1)
    if ready:
        lax.fori_loop(0, ready, add_hop, 0)
    lax.fori_loop(first, ticks + lags, tail, 0)

    if window == rows_out:
        gram_ref[...] = acc[...]
    else:
        inner_row = pl.multiple_of(in_block - lane0, 8)
        gram_ref[...] = acc[pl.ds(inner_row, rows_out), :]

    for k in range(1, n):
        z_copy(sbuf, 0, k, p).wait_send()
        for step in range(ITERS):
            z_copy(zbuf.at[step], step + 1, k, p).wait_send()
        z_copy(lbuf, ITERS + 1, k, p).wait_send()
    for k in range(1, nq):
        for phase in range(ITERS + 1):
            x_copy(xbuf.at[phase], phase, k, q).wait_send()
        x_copy(fbuf, ITERS + 1, k, q).wait_send()

    def drain_bulk(t, carry):
        for way, block, good in sends(t):
            @pl.when(good)
            def _():
                bulk(way, t, block).wait_send()
        return carry

    lax.fori_loop(0, ticks, drain_bulk, 0)

    def drain_rows(i, carry):
        block, c = lax.div(i, chunks), lax.rem(i, chunks)

        @pl.when(is_owner)
        def _():
            for peer in first_peers:
                row_first(block, c, peer).wait_send()

        @pl.when(is_relay)
        def _():
            for peer in again_peers:
                row_again(block, c, peer).wait_send()

        return carry

    lax.fori_loop(0, n * chunks, drain_rows, 0)


def per_device(sizes, energies, counts, labels):
    n, n_st, n_sub = sizes
    nq = n_st * n_sub
    samples, width = energies.shape
    rows_out = width * nq // n
    window = max(rows_out, LANES)
    chunks = 6 if n <= 8 else 1
    f32 = jnp.float32
    vmem = pl.BlockSpec(memory_space=pltpu.VMEM)
    dma = pltpu.SemaphoreType.DMA
    start, free, gram = pl.pallas_call(
        functools.partial(kernel, n, n_st, n_sub, chunks, rows_out),
        out_shape=(
            jax.ShapeDtypeStruct((1, width), f32),
            jax.ShapeDtypeStruct((1, width), f32),
            jax.ShapeDtypeStruct((rows_out, width), f32),
        ),
        in_specs=[pl.BlockSpec(memory_space=pl.ANY), vmem, vmem],
        out_specs=(vmem, vmem, vmem),
        scratch_shapes=[
            pltpu.VMEM((n, samples, width), f32),
            pltpu.VMEM((n, samples, window), f32),
            pltpu.VMEM((window, width), f32),
            pltpu.VMEM((n, 2, width), f32),
            pltpu.VMEM((ITERS, n, 1, width), f32),
            pltpu.VMEM((ITERS + 1, nq, 1, samples), f32),
            pltpu.VMEM((nq, 1, width), f32),
            pltpu.VMEM((n, 1, samples), f32),
            dma,
            dma((ITERS + 2, n)),
            dma((ITERS + 2, n)),
            dma((ITERS + 2, nq)),
            dma((ITERS + 2, nq)),
            dma((2, (n - 1) * chunks)),
            dma((2, (n - 1) * chunks)),
            dma((n_st + n_sub - 2, n, chunks)),
            dma((n, chunks)),
        ],
        compiler_params=pltpu.CompilerParams(
            collective_id=0, has_side_effects=True, vmem_limit_bytes=56 * 1024 * 1024
        ),
    )(energies, counts.reshape(1, width), labels.reshape(1, samples))
    scale = jnp.float32(width * nq) * counts.astype(f32)
    return start.reshape(width), free.reshape(width), scale[None, :] * gram


def solution(mesh):
    sizes = (mesh.shape["smp"], mesh.shape["st"], mesh.shape["sub"])
    return jax.shard_map(
        functools.partial(per_device, sizes),
        mesh=mesh,
        in_specs=(P(("grp", "smp"), ("st", "sub")), P(("grp", "st", "sub")), P(("grp", "smp"))),
        out_specs=(
            P(("grp", "st", "sub")),
            P(("grp", "st", "sub")),
            P(("grp", "smp"), ("st", "sub")),
        ),
        check_vma=False,
    )
```

time: 259 us -> 79.9 us (0.31)
  blocking collectives: 115 us -> 0 us
  waiting for transfers between devices: 104 us -> 0 us
  Pallas kernels: 0 us -> 74.2 us
  between operations: 14.1 us -> 0.66 us
  other arithmetic: 12.5 us -> 2.33 us
  matrix products: 9.84 us -> 0 us
    reduce_scatter x1 -> x0, waiting for transfers between devices: 77.4 us -> none  [per_device(): lax.psum_scatter(lax.dot_general(all_states, weights, (((0,), (0,)), ((),...]
    pallas_call x0 -> x1, Pallas kernels: none -> 74.2 us  [per_device(): pl.pallas_call(functools.partial(kernel, n, n_st, n_sub, chunks, rows_out...]
    pmax x7 -> x0, blocking collectives: 58.3 us -> none  [the longest x4 38.4 us: sample_lse(): row_peak = lax.pmax(local_peak, ('st', 'sub'))]
    psum x8 -> x0, blocking collectives: 57.1 us -> none  [the longest x3 24.2 us: state_lse(): lax.psum(jnp.sum(jnp.exp(scores - col_peak[None, :]), axis=0), 'smp')]
    all_gather x1 -> x0, waiting for transfers between devices: 26.9 us -> none  [per_device(): all_states = lax.all_gather(weights, ('st', 'sub'), axis=1, tiled=True)]
    dot_general x1 -> x0, matrix products: 9.84 us -> none  [per_device(): lax.dot_general(all_states, weights, (((0,), (0,)), ((), ())), precision=...]
    reduce_sum x8 -> x0, other arithmetic: 4.41 us -> none  [the longest x4 2.3 us: sample_lse(): jnp.sum(jnp.exp(scores - row_peak[:, None]), axis=1)]
    reduce_max x7 -> x0, other arithmetic: 3.34 us -> none  [the longest x4 1.75 us: sample_lse(): local_peak = jnp.max(scores, axis=1)]
  transfers between devices with their start and end apart: 2 -> 0, of which waited for: 2 -> 0; matrix products, arithmetic and copies ran while one was open for 0% -> 0% of each run, Pallas kernels for 0% -> 0%
where the time goes in v1:
time: 79.9 us; the launch traced here: 79.7 us
  Pallas kernels  74.2 us (93%)
  local copies, waits for them, and re-layouts  2.52 us (3%)
  other arithmetic  2.33 us (3%)
    pallas_call x1, Pallas kernels, per_device(): pl.pallas_call(functools.partial(kernel, n, n_st, n_sub, chunks, rows_out...  74.2 us
    mul x1, other arithmetic, per_device(): return (start.reshape(width), free.reshape(width), scale[None, :] * gram)  2.33 us

profile of v1, /device:TPU:3, one launch (start us, length us, event | category | flops | bytes accessed | tf_op | source)
XLA Modules:
  0.0 79.7 jit_solution(12763529566771261145)
XLA Ops:
  0.6 0.0 copy-start
  0.6 1.3 %reshape.20.labels_ref = s32[1,384]{1,0:T(1,128)} reshape(s32[384]{0:T(512)} %param.5) | data formatting | bytes 3072 | tf_op jit(solution)/shard_map/reshape | solution.py:394
  1.9 0.0 copy-done
  1.9 74.2 %shard_map.58 = (f32[1,512]{1,0:T(1,128)}, f32[1,512]{1,0:T(1,128)}, f32[512,512]{1,0:T(8,128)}) custom-call(f32[384,512]{1,0:T(8,128)} %e_hbm.1, s32[1,512]{1,0:T(1,128)} %bitcast.3, s32[1,384]{1,0:T(1,128)} %reshape.20.labels_ref), custom_call_target="tpu_custom_call" | custom-call | tf_op jit(solution)/shard_map/pallas_call | solution.py:363
  76.1 0.0 copy-start.2
  76.1 2.3 %broadcast_multiply_fusion = f32[512,512]{1,0:T(8,128)} fusion(f32[512,512]{1,0:T(8,128)} %get-tuple-element.8, f32[512]{0:T(512)S(1)} %convert_multiply_fusion), kind=kLoop, calls=%fused_computation | loop fusion | flops 262144 | bytes 2099200 | tf_op jit(solution)/shard_map/mul | solution.py:396
  78.4 0.0 copy-done.2
  78.4 0.0 copy-start.1
  78.4 0.6 copy.8
  79.0 0.1 copy-done.1
  79.1 0.6 copy.9
  (1 shorter events, 0.0 us)
Async XLA Ops:
  0.6 1.3 %copy-start = (s32[512]{0:T(512)S(1)}, s32[512]{0:T(512)}, u32[]{:S(2)}) copy-start(s32[512]{0:T(512)} %param.4) | copy-start | bytes 6148
  76.1 2.3 %copy-start.2 = (f32[1,512]{1,0:T(1,128)S(1)}, f32[1,512]{1,0:T(1,128)}, u32[]{:S(2)}) copy-start(f32[1,512]{1,0:T(1,128)} %get-tuple-element.6) | copy-start | bytes 6148
  78.4 0.7 copy-start.1

commit v2 on v1

--- a/solution.py
+++ b/solution.py
@@ -9,7 +9,8 @@
 
 ITERS = 3
 LANES = 128
-HAND, RELAY, LAND = 2, 2, 1
+HAND, RELAY, LAND = 4, 4, 1
+CHUNKS, HEAD, ZT, XT = 8, 3, 3, 1
 MESH = pl.DeviceIdType.MESH
 
 
@@ -210,15 +211,20 @@
 
     plan = iter(range(10**6))
 
+    def ticks_now(count):
+        for _ in range(count):
+            tick(next(plan))
+
+    ticks_now(HEAD)
+
     energies = eall.at[p]
-    label_rows = to_rows(labels_ref[...].astype(jnp.float32), width)
+    label_rows = to_rows(labels_ref[...].astype(jnp.float32).reshape(1, samples), width)
     state_ids = lax.broadcasted_iota(jnp.int32, (samples, width), 1) + q * width
     hit = label_rows == state_ids.astype(jnp.float32)
     sbuf[p, 0:1, :] = jnp.sum(jnp.where(hit, energies[...], jnp.float32(0.0)), axis=0, keepdims=True)
     sbuf[p, 1:2, :] = jnp.sum(hit.astype(jnp.float32), axis=0, keepdims=True)
     z_send(sbuf, 0)
-    tick(next(plan))
-    tick(next(plan))
+    ticks_now(ZT)
     log_counts = jnp.log(counts_ref[...].astype(jnp.float32))
     z_recv(sbuf, 0)
     total = sum(sbuf[j] for j in range(n))
@@ -232,7 +238,7 @@
         here = xbuf.at[phase]
         here[q] = to_lanes(local)
         x_send(here, phase)
-        tick(next(plan))
+        ticks_now(XT)
         x_recv(here, phase)
         return lse_of([here[j] for j in range(nq)])
 
@@ -245,7 +251,7 @@
         here = zbuf.at[step]
         here[p] = local
         z_send(here, step + 1)
-        tick(next(plan))
+        ticks_now(ZT)
         z_recv(here, step + 1)
         free = -lse_of([here[j] for j in range(n)])
     free_ref[...] = free
@@ -254,7 +260,7 @@
     denom = row_lse(free, ITERS)
     lbuf[p] = denom
     z_send(lbuf, ITERS + 1)
-    tick(next(plan))
+    ticks_now(ZT)
     acc[...] = jnp.zeros_like(acc)
     x_recv(fbuf, ITERS + 1)
     z_recv(lbuf, ITERS + 1)
@@ -356,7 +362,7 @@
     samples, width = energies.shape
     rows_out = width * nq // n
     window = max(rows_out, LANES)
-    chunks = 6 if n <= 8 else 1
+    chunks = CHUNKS
     f32 = jnp.float32
     vmem = pl.BlockSpec(memory_space=pltpu.VMEM)
     dma = pltpu.SemaphoreType.DMA
@@ -391,7 +397,7 @@
         compiler_params=pltpu.CompilerParams(
             collective_id=0, has_side_effects=True, vmem_limit_bytes=56 * 1024 * 1024
         ),
-    )(energies, counts.reshape(1, width), labels.reshape(1, samples))
+    )(energies, counts.reshape(1, width), labels)
     scale = jnp.float32(width * nq) * counts.astype(f32)
     return start.reshape(width), free.reshape(width), scale[None, :] * gram
 

time: 79.9 us -> 71.8 us (0.90)
  Pallas kernels: 74.2 us -> 66.7 us
  local copies, waits for them, and re-layouts: 2.52 us -> 1.26 us
    pallas_call x1, Pallas kernels: 74.2 us -> 66.7 us  [per_device(): pl.pallas_call(functools.partial(kernel, n, n_st, n_sub, chunks, rows_out...]
    reshape x1 -> x0, local copies, waits for them, and re-layouts: 1.25 us -> none  [per_device(): labels.reshape(1, samples)]
where the time goes in v2:
time: 71.8 us; the launch traced here: 71.6 us
  Pallas kernels  66.7 us (93%)
  other arithmetic  3.02 us (4%)
  local copies, waits for them, and re-layouts  1.26 us (2%)
    pallas_call x1, Pallas kernels, per_device(): pl.pallas_call(functools.partial(kernel, n, n_st, n_sub, chunks, rows_out...  66.7 us
    mul x1, other arithmetic, per_device(): return (start.reshape(width), free.reshape(width), scale[None, :] * gram)  2.33 us

profile of v2, /device:TPU:3, one launch (start us, length us, event | category | flops | bytes accessed | tf_op | source)
XLA Modules:
  0.0 71.6 jit_solution(13835146014371162135)
XLA Ops:
  0.6 0.7 convert_multiply_fusion
  1.3 66.7 %shard_map.58 = (f32[1,512]{1,0:T(1,128)}, f32[1,512]{1,0:T(1,128)}, f32[512,512]{1,0:T(8,128)}) custom-call(f32[384,512]{1,0:T(8,128)} %e_hbm.1, s32[1,512]{1,0:T(1,128)} %bitcast.3, s32[384]{0:T(512)} %labels_ref.1), custom_call_target="tpu_custom_call" | custom-call | tf_op jit(solution)/shard_map/pallas_call | solution.py:369
  68.0 0.0 copy-start.1
  68.0 2.3 %broadcast_multiply_fusion = f32[512,512]{1,0:T(8,128)} fusion(f32[512,512]{1,0:T(8,128)} %get-tuple-element.8, f32[512]{0:T(512)S(1)} %convert_multiply_fusion), kind=kLoop, calls=%fused_computation | loop fusion | flops 262144 | bytes 2099200 | tf_op jit(solution)/shard_map/mul | solution.py:402
  70.3 0.0 copy-done.1
  70.3 0.0 copy-start
  70.3 0.6 copy.8
  70.9 0.1 copy-done
  71.0 0.6 copy.9
Async XLA Ops:
  68.0 2.3 %copy-start.1 = (f32[1,512]{1,0:T(1,128)S(1)}, f32[1,512]{1,0:T(1,128)}, u32[]{:S(2)}) copy-start(f32[1,512]{1,0:T(1,128)} %get-tuple-element.6) | copy-start | bytes 6148
  70.3 0.7 copy-start

commit v3 on v2

--- a/solution.py
+++ b/solution.py
@@ -10,7 +10,7 @@
 ITERS = 3
 LANES = 128
 HAND, RELAY, LAND = 4, 4, 1
-CHUNKS, HEAD, ZT, XT = 8, 3, 3, 1
+CHUNKS, HEAD, ZT, XT = 8, 4, 3, 1
 MESH = pl.DeviceIdType.MESH
 
 
@@ -187,14 +187,16 @@
             def _():
                 for peer in first_peers:
                     row_first(block, c, peer).start()
-                row_local(block, c).start()
+                if window != width:
+                    row_local(block, c).start()
 
         u2 = u - RELAY
         c2 = lax.rem(u2 + 2 * chunks, chunks)
         for way, block, good in events(u2):
-            @pl.when(jnp.logical_and(good, is_owner))
-            def _():
-                row_local(block, c2).wait()
+            if window != width:
+                @pl.when(jnp.logical_and(good, is_owner))
+                def _():
+                    row_local(block, c2).wait()
 
             @pl.when(jnp.logical_and(good, is_relay))
             def _():
@@ -265,7 +267,7 @@
     x_recv(fbuf, ITERS + 1)
     z_recv(lbuf, ITERS + 1)
 
-    def add_block(block):
+    def add_block(block, rows):
         denom_rows = to_rows(lbuf[block], LANES)
         row_free = fbuf[owner] if window == width else fbuf[owner, :, pl.ds(lane0, window)]
 
@@ -276,7 +278,7 @@
             )
 
         col_high, col_low = weights(free_ref[...], eall.at[block])
-        row_high, row_low = weights(row_free, erow.at[block])
+        row_high, row_low = weights(row_free, rows.at[block])
         acc[...] += pairs(row_high, col_high) + (
             pairs(row_high, col_low) + pairs(row_low, col_high)
         )
@@ -290,7 +292,16 @@
 
             @pl.when(good)
             def _():
-                add_block(block)
+                if window != width:
+                    add_block(block, erow)
+                else:
+                    @pl.when(is_owner)
+                    def _():
+                        add_block(block, eall)
+
+                    @pl.when(jnp.logical_not(is_owner))
+                    def _():
+                        add_block(block, erow)
 
             return inner
 

time: 71.8 us -> 71.9 us (level)
  no operation moved by 1% of the time
where the time goes in v3:
time: 71.9 us; the launch traced here: 71.7 us
  Pallas kernels  66.8 us (93%)
  other arithmetic  3.02 us (4%)
  local copies, waits for them, and re-layouts  1.26 us (2%)
    pallas_call x1, Pallas kernels, per_device(): pl.pallas_call(functools.partial(kernel, n, n_st, n_sub, chunks, rows_out...  66.8 us
    mul x1, other arithmetic, per_device(): return (start.reshape(width), free.reshape(width), scale[None, :] * gram)  2.33 us

profile of v3, /device:TPU:3, one launch (start us, length us, event | category | flops | bytes accessed | tf_op | source)
XLA Modules:
  0.0 71.7 jit_solution(17519552997710232539)
XLA Ops:
  0.6 0.7 convert_multiply_fusion
  1.3 66.8 %shard_map.58 = (f32[1,512]{1,0:T(1,128)}, f32[1,512]{1,0:T(1,128)}, f32[512,512]{1,0:T(8,128)}) custom-call(f32[384,512]{1,0:T(8,128)} %e_hbm.1, s32[1,512]{1,0:T(1,128)} %bitcast.3, s32[384]{0:T(512)} %labels_ref.1), custom_call_target="tpu_custom_call" | custom-call | tf_op jit(solution)/shard_map/pallas_call | solution.py:380
  68.1 0.0 copy-start.1
  68.1 2.3 %broadcast_multiply_fusion = f32[512,512]{1,0:T(8,128)} fusion(f32[512,512]{1,0:T(8,128)} %get-tuple-element.8, f32[512]{0:T(512)S(1)} %convert_multiply_fusion), kind=kLoop, calls=%fused_computation | loop fusion | flops 262144 | bytes 2099200 | tf_op jit(solution)/shard_map/mul | solution.py:413
  70.4 0.0 copy-done.1
  70.4 0.0 copy-start
  70.4 0.6 copy.8
  71.0 0.1 copy-done
  71.1 0.6 copy.9
Async XLA Ops:
  68.1 2.3 %copy-start.1 = (f32[1,512]{1,0:T(1,128)S(1)}, f32[1,512]{1,0:T(1,128)}, u32[]{:S(2)}) copy-start(f32[1,512]{1,0:T(1,128)} %get-tuple-element.6) | copy-start | bytes 6148
  70.4 0.7 copy-start
